TPU v7x, 32 devices: a whole 2x2x4 slice. The times are simulated.
32 devices in a mesh: dp: 8 (over y, x, core), context: 4 (over z).
Axes of the slice: x: 2, y: 2, z: 4, core: 2. Of those that a mesh axis runs over, the one named last changes fastest.
Arguments:
- image_tokens: bfloat16 [8, 448, 3072], P('dp', 'context'), may hold values from -6 to 6
- text_tokens: bfloat16 [8, 64, 3072], P('dp', 'context'), may hold values from -6 to 6
- image_mod: bfloat16 [8, 3, 3072], P('dp'), may hold values from -4 to 4
- text_mod: bfloat16 [8, 3, 3072], P('dp'), may hold values from -4 to 4
- image_qkv_weight: bfloat16 [3072, 3, 16, 128], P('dp', None, 'context'), may hold values from -0.109375 to 0.109375
- text_qkv_weight: bfloat16 [3072, 3, 16, 128], P('dp', None, 'context'), may hold values from -0.109375 to 0.109375
- image_out_weight: bfloat16 [3072, 16, 128], P('dp', 'context'), may hold values from -1 to 1
- text_out_weight: bfloat16 [3072, 16, 128], P('dp', 'context'), may hold values from -1 to 1
- image_slope: bfloat16 [8, 448, 3072], P('dp', 'context'), may hold values from -0.119628906 to 0.119628906
- text_slope: bfloat16 [8, 64, 3072], P('dp', 'context'), may hold values from -0.119628906 to 0.119628906
Outputs:
- image_update: bfloat16 [8, 448, 3072], P('dp', 'context')
- text_update: bfloat16 [8, 64, 3072], P('dp', 'context')
- image_qkv_grad: float32 [3072, 3, 16, 128], P('dp', None, 'context')
- text_qkv_grad: float32 [3072, 3, 16, 128], P('dp', None, 'context')
- image_out_grad: float32 [3072, 16, 128], P('dp', 'context')
- text_out_grad: float32 [3072, 16, 128], P('dp', 'context')
- image_mod_grad: float32 [8, 3, 3072], P('dp')
- text_mod_grad: float32 [8, 3, 3072], P('dp')
All inputs are finite; a program needn't handle non-finite values.
Results may differ from a plain program's by a relative error of at most 0.015.
Values may be sent and summed in bfloat16 or wider, within the bound.
No kernel may reach another device: no remote copies, remote signals or barrier semaphores. Data moves between devices by JAX's collectives and lax.ppermute only.
A program may use at most 128 MiB of HBM per device.

v0:
```python
import jax
import jax.numpy as jnp
from jax import lax
from jax.sharding import PartitionSpec as P

norm_eps = 1e-06


def layer_normal(values):
    average = jnp.mean(values, axis=-1, keepdims=True)
    centred = values - average
    return centred * lax.rsqrt(jnp.mean(centred * centred, axis=-1, keepdims=True) + norm_eps)


def rms_normal(values):
    factor = lax.rsqrt(jnp.mean(values * values, axis=-1, keepdims=True) + norm_eps)
    return (values * factor, factor)


def rms_back(normed, factor, slopes):
    return factor * (slopes - normed * jnp.mean(slopes * normed, axis=-1, keepdims=True))


def modulate(tokens, modulation):
    normal = layer_normal(tokens.astype(jnp.float32))
    factors = modulation.astype(jnp.float32)
    return (normal, ((1.0 + factors[1]) * normal + factors[0]).astype(jnp.bfloat16))


def contract_rows(left_side, right_side):
    return lax.dot_general(
        left_side, right_side, (((0,), (0,)), ((), ())), preferred_element_type=jnp.float32
    )


def contract_last(left_side, right_side):
    return lax.dot_general(
        left_side, right_side, (((1,), (1,)), ((), ())), preferred_element_type=jnp.float32
    )


def body(
    image_tokens,
    text_tokens,
    image_mod,
    text_mod,
    image_qkv_weight,
    text_qkv_weight,
    image_out_weight,
    text_out_weight,
    image_slope,
    text_slope,
):
    groups = lax.axis_size("context")
    own_image = image_tokens.shape[1]
    own_text = text_tokens.shape[1]
    block_rows = own_image + own_text
    model_width = image_tokens.shape[2]
    shard_rows = image_qkv_weight.shape[0]
    head_count = image_qkv_weight.shape[2]
    head_size = image_qkv_weight.shape[3]
    inner_width = head_count * head_size
    triple = 3 * inner_width
    text_rows = own_text * groups
    score_scale = head_size ** (-0.5)
    whole_image, whole_text, slopes_image, slopes_text = (
        lax.all_gather(image_tokens, "context", axis=1, tiled=True),
        lax.all_gather(text_tokens, "context", axis=1, tiled=True),
        lax.all_gather(image_slope, "context", axis=1, tiled=True),
        lax.all_gather(text_slope, "context", axis=1, tiled=True),
    )
    full_q_image, full_q_text, full_o_image, full_o_text = (
        lax.all_gather(image_qkv_weight, "dp", axis=0, tiled=True),
        lax.all_gather(text_qkv_weight, "dp", axis=0, tiled=True),
        lax.all_gather(image_out_weight, "dp", axis=0, tiled=True),
        lax.all_gather(text_out_weight, "dp", axis=0, tiled=True),
    )
    wq_image = full_q_image.reshape(model_width, triple)
    wq_text = full_q_text.reshape(model_width, triple)
    wo_image = full_o_image.reshape(model_width, inner_width)
    wo_text = full_o_text.reshape(model_width, inner_width)
    normal_image, input_image = modulate(whole_image[0], image_mod[0])
    normal_text, input_text = modulate(whole_text[0], text_mod[0])
    projected = jnp.concatenate(
        [
            jnp.dot(input_text, wq_text, preferred_element_type=jnp.float32),
            jnp.dot(input_image, wq_image, preferred_element_type=jnp.float32),
        ],
        axis=0,
    )
    projected = projected.reshape(-1, 3, head_count, head_size)
    query_normal, query_factor = rms_normal(projected[:, 0])
    key_normal, key_factor = rms_normal(projected[:, 1])
    query_b = query_normal.astype(jnp.bfloat16)
    key_b = key_normal.astype(jnp.bfloat16)
    value_b = projected[:, 2].astype(jnp.bfloat16)
    scores = (
        jnp.einsum("ihe,jhe->hij", query_b, key_b, preferred_element_type=jnp.float32) * score_scale
    )
    raised = jnp.exp(scores)
    attn_probs = raised / jnp.sum(raised, axis=-1, keepdims=True)
    probs_b = attn_probs.astype(jnp.bfloat16)
    attended = jnp.einsum(
        "hij,jhe->ihe", probs_b, value_b, preferred_element_type=jnp.float32
    ).astype(jnp.bfloat16)
    flat_att = attended.reshape(-1, inner_width)
    att_text = flat_att[:text_rows]
    att_image = flat_att[text_rows:]
    blocks_text = att_text.reshape(groups, own_text, inner_width)
    blocks_image = att_image.reshape(groups, own_image, inner_width)
    block_count = block_rows * lax.axis_size("context") // block_rows
    part_text = blocks_text.reshape(block_count * own_text, inner_width)
    part_image = blocks_image.reshape(block_count * own_image, inner_width)
    out_text = contract_last(part_text, wo_text).reshape(block_count, own_text, model_width)
    out_image = contract_last(part_image, wo_image).reshape(block_count, own_image, model_width)
    mixed_rows = lax.psum_scatter(
        jnp.concatenate([out_text, out_image], axis=1)
        .reshape(block_rows * lax.axis_size("context"), model_width)
        .astype(jnp.bfloat16),
        "context",
        scatter_dimension=0,
        tiled=True,
    ).astype(jnp.float32)
    mixed_text = mixed_rows[:own_text]
    mixed_image = mixed_rows[own_text:]
    factors_image = image_mod[0].astype(jnp.float32)
    factors_text = text_mod[0].astype(jnp.float32)
    update_image = (factors_image[2] * mixed_image).astype(jnp.bfloat16)[None]
    update_text = (factors_text[2] * mixed_text).astype(jnp.bfloat16)[None]
    gate_part_image = jnp.sum(image_slope[0].astype(jnp.float32) * mixed_image, axis=0)
    gate_part_text = jnp.sum(text_slope[0].astype(jnp.float32) * mixed_text, axis=0)
    gated_image = (factors_image[2] * slopes_image[0].astype(jnp.float32)).astype(jnp.bfloat16)
    gated_text = (factors_text[2] * slopes_text[0].astype(jnp.float32)).astype(jnp.bfloat16)
    back_att = jnp.concatenate(
        [
            jnp.dot(gated_text, wo_text, preferred_element_type=jnp.float32),
            jnp.dot(gated_image, wo_image, preferred_element_type=jnp.float32),
        ],
        axis=0,
    )
    back_att = back_att.astype(jnp.bfloat16).reshape(-1, head_count, head_size)
    back_probs = jnp.einsum("ihe,jhe->hij", back_att, value_b, preferred_element_type=jnp.float32)
    back_value = jnp.einsum("hij,ihe->jhe", probs_b, back_att, preferred_element_type=jnp.float32)
    back_scores = (
        attn_probs
        * (back_probs - jnp.sum(attn_probs * back_probs, axis=-1, keepdims=True))
        * score_scale
    ).astype(jnp.bfloat16)
    back_query = jnp.einsum("hij,jhe->ihe", back_scores, key_b, preferred_element_type=jnp.float32)
    back_key = jnp.einsum("hij,ihe->jhe", back_scores, query_b, preferred_element_type=jnp.float32)
    back_qkv = (
        jnp.stack(
            [
                rms_back(query_normal, query_factor, back_query),
                rms_back(key_normal, key_factor, back_key),
                back_value,
            ],
            axis=1,
        )
        .reshape(-1, triple)
        .astype(jnp.bfloat16)
    )
    back_text = back_qkv[:text_rows]
    back_image = back_qkv[text_rows:]
    spread_image = contract_last(back_image, wq_image)
    spread_text = contract_last(back_text, wq_text)
    part_image = jnp.stack(
        [
            jnp.sum(spread_image, axis=0),
            jnp.sum(spread_image * normal_image, axis=0),
            gate_part_image,
        ]
    )
    part_text = jnp.stack(
        [jnp.sum(spread_text, axis=0), jnp.sum(spread_text * normal_text, axis=0), gate_part_text]
    )
    modsum_image, modsum_text = (
        lax.psum(part_image.astype(jnp.bfloat16), "context").astype(jnp.float32),
        lax.psum(part_text.astype(jnp.bfloat16), "context").astype(jnp.float32),
    )
    pieces = [contract_rows(input_image, back_image)]
    pieces.append(contract_rows(gated_image, att_image))
    pieces.append(contract_rows(gated_text, att_text))
    summed = lax.psum_scatter(
        jnp.concatenate(pieces, axis=1).astype(jnp.bfloat16), "dp", scatter_dimension=0, tiled=True
    ).astype(jnp.float32)
    grad_q_image = summed[:, :triple]
    remaining = summed[:, triple:]
    columns = lax.all_to_all(input_text[None], "dp", split_axis=2, concat_axis=0, tiled=True)
    slopes_all = lax.all_gather(back_text[None], "dp", axis=0, tiled=True)
    per_image = jnp.einsum("itd,itj->idj", columns, slopes_all, preferred_element_type=jnp.float32)
    rounded = lax.optimization_barrier(per_image.astype(jnp.bfloat16))
    grad_q_text = jnp.sum(rounded.astype(jnp.float32), axis=0)
    grad_o_image = remaining[:, :inner_width]
    grad_o_text = remaining[:, inner_width:]
    return (
        update_image,
        update_text,
        grad_q_image.reshape(shard_rows, 3, head_count, head_size),
        grad_q_text.reshape(shard_rows, 3, head_count, head_size),
        grad_o_image.reshape(shard_rows, head_count, head_size),
        grad_o_text.reshape(shard_rows, head_count, head_size),
        modsum_image[None],
        modsum_text[None],
    )


def solution(mesh):
    placed = (
        P("dp", "context", None),
        P("dp", "context", None),
        P("dp", None, None),
        P("dp", None, None),
        P("dp", None, "context", None),
        P("dp", None, "context", None),
        P("dp", "context", None),
        P("dp", "context", None),
        P("dp", "context", None),
        P("dp", "context", None),
    )
    return jax.shard_map(
        body,
        mesh=mesh,
        in_specs=placed,
        out_specs=(
            P("dp", "context", None),
            P("dp", "context", None),
            P("dp", None, "context", None),
            P("dp", None, "context", None),
            P("dp", "context", None),
            P("dp", "context", None),
            P("dp", None, None),
            P("dp", None, None),
        ),
        check_vma=False,
    )
```

profile of v0, /device:TPU:0, one launch (start us, length us, event | category | flops | bytes accessed | tf_op | source)
XLA Modules:
  0.0 606.1 jit_solution(18341433870807146927)
XLA Ops:
  11.3 19.2 %all_gather.27 = bf16[1,64,3072]{2,1,0:T(8,128)(2,1)S(1)} all-gather(bf16[1,16,3072]{2,1,0:T(8,128)(2,1)S(1)} %copy-done.28), channel_id=1, replica_groups=mesh['dp'=8,'context'=4] {'context'}, dimensions={1}, use_global_device_ids=true | all-gather | bytes 491520 | tf_op jit(solution)/shard_map/all_gather | solution.py:68
  30.9 19.6 %all_gather.33 = bf16[1,64,3072]{2,1,0:T(8,128)(2,1)} all-gather(bf16[1,16,3072]{2,1,0:T(8,128)(2,1)S(1)} %copy-done.23), channel_id=1, replica_groups=mesh['dp'=8,'context'=4] {'context'}, dimensions={1}, use_global_device_ids=true | all-gather | bytes 491520 | tf_op jit(solution)/shard_map/all_gather | solution.py:70
  52.8 24.9 %all-gather.10.cloned.1.call-done = bf16[1,448,3072]{2,1,0:T(8,128)(2,1)} async-done(((bf16[1,112,3072]{2,1,0:T(8,128)(2,1)}), bf16[1,448,3072]{2,1,0:T(8,128)(2,1)}) %all-gather.10.cloned.1.call-update) | async-done | bytes 2752528 | tf_op jit(solution)/shard_map/all_gather | solution.py:67
  77.6 2.4 convert_reduce_fusion.1
  81.7 29.0 %all-gather.14.cloned.1.call-done = bf16[3072,4,128]{2,1,0:T(4,128)(2,1)} async-done(((bf16[384,4,128]{2,1,0:T(4,128)(2,1)}), bf16[3072,4,128]{2,1,0:T(4,128)(2,1)}) %all-gather.14.cloned.1.call-update) | async-done | bytes 3145744 | tf_op jit(solution)/shard_map/all_gather | solution.py:76
  110.7 4.1 copy.103
  114.9 3.3 copy.88
  118.2 26.6 %all-gather.16.cloned.1.call-done = bf16[3072,4,128]{2,1,0:T(4,128)(2,1)} async-done(((bf16[384,4,128]{2,1,0:T(4,128)(2,1)}), bf16[3072,4,128]{2,1,0:T(4,128)(2,1)}) %all-gather.16.cloned.1.call-update) | async-done | bytes 3145744 | tf_op jit(solution)/shard_map/all_gather | solution.py:75
  144.8 4.1 copy.102
  149.0 4.6 copy.89
  153.6 2.7 convolution_convert_fusion.8
  156.3 46.9 %all-gather.18.cloned.1.call-done = bf16[1,448,3072]{2,1,0:T(8,128)(2,1)} async-done(((bf16[1,112,3072]{2,1,0:T(8,128)(2,1)}), bf16[1,448,3072]{2,1,0:T(8,128)(2,1)}) %all-gather.18.cloned.1.call-update) | async-done | bytes 2752528 | tf_op jit(solution)/shard_map/all_gather | solution.py:69
  203.2 5.1 fusion.49
  208.3 54.1 %all-gather.8.cloned.1.call-done = bf16[3072,3,4,128]{3,2,1,0:T(4,128)(2,1)} async-done(((bf16[384,3,4,128]{3,2,1,0:T(4,128)(2,1)}), bf16[3072,3,4,128]{3,2,1,0:T(4,128)(2,1)}) %all-gather.8.cloned.1.call-update) | async-done | bytes 9437200 | tf_op jit(solution)/shard_map/all_gather | solution.py:74
  262.4 16.2 %reshape.247 = bf16[3072,1536]{1,0:T(8,128)(2,1)} reshape(bf16[3072,3,4,128]{3,2,1,0:T(4,128)(2,1)} %all-gather.8.cloned.1.call-done) | data formatting | bytes 18874368 | tf_op jit(solution)/shard_map/reshape | solution.py:79
  278.6 5.4 fusion.78
  284.0 38.9 %all-gather.12.cloned.1.call-done = bf16[3072,3,4,128]{3,2,1,0:T(4,128)(2,1)} async-done(((bf16[384,3,4,128]{3,2,1,0:T(4,128)(2,1)}), bf16[3072,3,4,128]{3,2,1,0:T(4,128)(2,1)}) %all-gather.12.cloned.1.call-update) | async-done | bytes 9437200 | tf_op jit(solution)/shard_map/all_gather | solution.py:73
  322.9 15.9 %reshape.248 = bf16[3072,1536]{1,0:T(8,128)(2,1)} reshape(bf16[3072,3,4,128]{3,2,1,0:T(4,128)(2,1)} %all-gather.12.cloned.1.call-done) | data formatting | bytes 18874368 | tf_op jit(solution)/shard_map/reshape | solution.py:78
  338.8 7.6 %fusion.21 = f32[448,1536]{1,0:T(8,128)S(1)} fusion(bf16[3072,1536]{1,0:T(8,128)(2,1)} %reshape.248, bf16[1,448,3072]{2,1,0:T(8,128)(2,1)S(1)} %copy-done.1, f32[3072]{0:T(1024)} %bitcast.215, f32[448]{0:T(512)} %add_rsqrt_fusion.2, f32[448]{0:T(512)S(1)} %broadcast_multiply_fusion.2, f32[3072]{0:T(1024)} %bitcast.213), kind=kOutput, calls=%fused_computation.37 | convolution fusion | flops 4236115968 | bytes 14970368 | tf_op jit(solution)/shard_map/dot_general | solution.py:87
  346.4 1.9 pad_maximum_fusion.1
  348.3 2.4 copy.94
  351.0 3.7 fusion.80
  355.7 1.9 copy-done.10
  357.6 1.8 fusion.53
  359.4 8.2 %fusion.46 = f32[512,4,128]{0,2,1:T(8,128)} fusion(f32[4,512,512]{1,2,0:T(8,128)} %fusion.80, f32[512,3,4,128]{0,3,2,1:T(8,128)S(1)} %bitcast.182, f32[512,4]{0,1:T(4,128)} %copy-done.30, f32[4,512,512]{1,2,0:T(8,128)} %copy-done.10, f32[4,512]{1,0:T(4,128)} %copy-done.35), kind=kOutput, calls=%fused_computation.58 | convolution fusion | flops 278399488 | bytes 18898944 | tf_op jit(solution)/shard_map/hij,ihe->jhe/dot_general | solution.py:150
  367.6 10.0 %multiply_reduce_fusion.2 = (f32[512,4]{0,1:T(4,128)}, f32[512,4]{0,1:T(4,128)}, f32[512,4,128]{0,2,1:T(8,128)}) fusion(f32[512,3,4,128]{0,3,2,1:T(8,128)S(1)} %bitcast.183, f32[512,4]{0,1:T(4,128)} %copy-done.30, f32[512,4,128]{0,2,1:T(8,128)} %fusion.46, f32[512,4]{0,1:T(4,128)} %copy-done.29, f32[4,512,512]{1,2,0:T(8,128)} %fusion.80, ...), kind=kOutput, calls=%fused_computation.74 | convolution fusion | flops 279968256 | bytes 22077440 | tf_op jit(solution)/shard_map/hij,jhe->ihe/dot_general | solution.py:149
  379.0 2.0 fusion.71
  382.7 1.8 copy.75
  384.6 5.7 reshape.258
  390.3 5.8 reshape.259
  396.1 3.0 fusion.52
  399.8 1.1 slice.109
  400.9 1.6 copy.63
  402.5 1.5 dot_general.70
  404.0 2.2 reshape.263
  406.2 3.0 convolution_convert_fusion.5
  409.2 3.0 convolution_convert_fusion.4
  412.2 1.8 pad_maximum_fusion.2
  416.9 1.8 convolution_convert_fusion.3
  418.7 6.2 %convolution_convert_fusion = bf16[3072,1536]{0,1:T(8,128)(2,1)S(1)} fusion(bf16[448,1536]{0,1:T(8,128)(2,1)S(1)} %bitcast.202, bf16[1,448,3072]{2,1,0:T(8,128)(2,1)S(1)} %copy-done.2, f32[3072]{0:T(1024)S(1)} %bitcast.216, f32[448]{0:T(512)S(1)} %copy-done.38, f32[3072]{0:T(1024)S(1)} %bitcast.214, f32[448]{0:T(512)S(1)} %broadcast_multiply_fusion.2), kind=kOutput, calls=%fused_computation.3 | convolution fusion | flops 4240834560 | bytes 13594112 | tf_op jit(solution)/shard_map/dot_general | solution.py:31
  424.9 7.6 %pad_maximum_fusion = bf16[3072,2560]{0,1:T(8,128)(2,1)} fusion(bf16[3072,512]{0,1:T(8,128)(2,1)S(1)} %convolution_convert_fusion.2, bf16[3072,512]{0,1:T(8,128)(2,1)S(1)} %convolution_convert_fusion.3, bf16[3072,1536]{0,1:T(8,128)(2,1)S(1)} %convolution_convert_fusion), kind=kLoop, calls=%fused_computation.2 | loop fusion | flops 47185920 | bytes 31457280 | tf_op jit(solution)/shard_map/concatenate | solution.py:185
  432.5 20.1 %copy.92 = bf16[3072,2560]{1,0:T(8,128)(2,1)} copy(bf16[3072,2560]{0,1:T(8,128)(2,1)} %pad_maximum_fusion) | data formatting | bytes 31457280
  453.6 2.9 copy.72
  457.0 18.9 %reduce.2 = bf16[3072,64]{1,0:T(8,128)(2,1)} reduce(bf16[3072,1,64]{2,1,0:T(2,128)(2,1)} %bitcast.193, bf16[]{:T(256)} %broadcast.209), dimensions={1}, to_apply=%bitcast.152.reduce_sub_computation | reduce | bytes 786434
  475.9 2.7 reshape.268
  478.6 12.6 %all_to_all.18 = bf16[8,2,12288]{2,1,0:T(2,128)(2,1)} all-to-all(bf16[8,2,12288]{2,1,0:T(2,128)(2,1)} %reshape.268), channel_id=1, replica_groups=mesh['dp'=8,'context'=4] {'dp'}, dimensions={0} | all-to-all | bytes 786432 | tf_op jit(solution)/shard_map/all_to_all | solution.py:189
  491.2 3.7 reshape.269
  495.0 2.7 copy.95
  497.6 2.4 copy.74
  500.1 7.3 %fusion.103 = (bf16[3072]{0:T(1024)(128)(2,1)S(1)}, bf16[3072]{0:T(1024)(128)(2,1)S(1)}) fusion(f32[64]{0:T(128)} %copy-done.37, f32[64]{0:T(128)} %copy-done.36, bf16[1,64,3072]{2,1,0:T(8,128)(2,1)S(1)} %all_gather.27, bf16[64,1536]{0,1:T(8,128)(2,1)S(1)} %bitcast.196, bf16[3072,1536]{1,0:T(8,128)(2,1)} %reshape.247), kind=kOutput, calls=%fused_computation.131 | convolution fusion | flops 605153280 | bytes 10039808 | tf_op jit(solution)/shard_map/dot_general | solution.py:37
  507.5 9.5 %fusion.102 = (bf16[3072]{0:T(1024)(128)(2,1)S(1)}, bf16[3072]{0:T(1024)(128)(2,1)S(1)}) fusion(f32[448]{0:T(512)S(1)} %copy-done.39, f32[448]{0:T(512)S(1)} %broadcast_multiply_fusion.2, bf16[1,448,3072]{2,1,0:T(8,128)(2,1)S(1)} %copy-done.2, bf16[448,1536]{0,1:T(8,128)(2,1)S(1)} %bitcast.203, bf16[3072,1536]{1,0:T(8,128)(2,1)} %reshape.248), kind=kOutput, calls=%fused_computation.130 | convolution fusion | flops 4236109824 | bytes 13581824 | tf_op jit(solution)/shard_map/dot_general | solution.py:37
  517.0 4.0 convolution_convert_fusion.1
  521.1 1.3 convert_reduce_fusion
  522.4 1.9 reshape.253
  524.3 1.3 convert_element_type.146
  526.3 1.1 fusion.42
  527.6 19.2 %all-reduce = (bf16[1,3,3072]{2,0,1:T(2,128)(2,1)S(1)}, bf16[1,3,3072]{2,0,1:T(2,128)(2,1)S(1)}) all-reduce(bf16[1,3,3072]{2,0,1:T(2,128)(2,1)S(1)} %broadcast_in_dim.37, bf16[1,3,3072]{2,0,1:T(2,128)(2,1)S(1)} %broadcast_in_dim.39), channel_id=1, replica_groups=mesh['dp'=8,'context'=4] {'context'}, use_global_device_ids=true, to_apply=%region_16.0 | all-reduce | flops 18432 | bytes 73728 | tf_op jit(solution)/shard_map/psum | solution.py:178
  548.1 39.9 %reduce-scatter.7.cloned.1.call-done = bf16[384,2560]{1,0:T(8,128)(2,1)} async-done(((bf16[3072,2560]{1,0:T(8,128)(2,1)}), bf16[384,2560]{1,0:T(8,128)(2,1)}) %reduce-scatter.7.cloned.1.call-update) | async-done | bytes 1966096
  588.0 2.8 copy.93
  590.8 1.0 fusion.104
  591.8 1.6 slice.114
  593.4 2.4 copy.78
  595.8 1.1 copy.77
  596.9 2.4 copy.76
  (139 shorter events, 19.9 us)
Async XLA Ops:
  7.2 4.0 copy-start.26
  7.2 4.1 copy-start.27
  7.2 4.1 copy-start.28
  7.2 23.7 %copy-start.23 = (bf16[1,16,3072]{2,1,0:T(8,128)(2,1)S(1)}, bf16[1,16,3072]{2,1,0:T(8,128)(2,1)}, u32[]{:S(2)}) copy-start(bf16[1,16,3072]{2,1,0:T(8,128)(2,1)} %param.19) | copy-start | bytes 294916
  7.2 70.4 %all-gather.10.cloned.1.call-start = ((), (), s32[]{:S(2)}) async-start(), calls=%async_computation.4 | async-start | bytes 3440640 | tf_op jit(solution)/shard_map/all_gather | solution.py:67
  7.9 102.8 %all-gather.14.cloned.1.call-start = ((), (), s32[]{:S(2)}) async-start(), calls=%async_computation.6 | async-start | bytes 3538944 | tf_op jit(solution)/shard_map/all_gather | solution.py:76
  8.7 136.1 %all-gather.16.cloned.1.call-start = ((), (), s32[]{:S(2)}) async-start(), calls=%async_computation.7 | async-start | bytes 3538944 | tf_op jit(solution)/shard_map/all_gather | solution.py:75
  9.4 193.8 %all-gather.18.cloned.1.call-start = ((), (), s32[]{:S(2)}) async-start(), calls=%async_computation.9 | async-start | bytes 3440640 | tf_op jit(solution)/shard_map/all_gather | solution.py:69
  10.0 252.4 %all-gather.8.cloned.1.call-start = ((), (), s32[]{:S(2)}) async-start(), calls=%async_computation.3 | async-start | bytes 10616832 | tf_op jit(solution)/shard_map/all_gather | solution.py:74
  10.6 312.3 %all-gather.12.cloned.1.call-start = ((), (), s32[]{:S(2)}) async-start(), calls=%async_computation.5 | async-start | bytes 10616832 | tf_op jit(solution)/shard_map/all_gather | solution.py:73
  11.2 505.8 %all-gather.20.cloned.1.call-start = ((), (), s32[]{:S(2)}) async-start(), calls=%async_computation.10 | async-start | bytes 1769472 | tf_op jit(solution)/shard_map/all_gather | solution.py:190
  30.6 84.2 %copy-start.36 = (f32[64]{0:T(128)}, f32[64]{0:T(128)S(1)}, u32[]{:S(2)}) copy-start(f32[64]{0:T(128)S(1)} %broadcast_multiply_fusion.3) | copy-start | bytes 772
  50.5 64.4 %copy-start.37 = (f32[64]{0:T(128)}, f32[64]{0:T(128)S(1)}, u32[]{:S(2)}) copy-start(f32[64]{0:T(128)S(1)} %add_rsqrt_fusion.3) | copy-start | bytes 772
  77.6 2.6 copy-start
  208.3 70.3 %copy-start.4 = (bf16[1,64,3072]{2,1,0:T(8,128)(2,1)S(1)}, bf16[1,64,3072]{2,1,0:T(8,128)(2,1)}, u32[]{:S(2)}) copy-start(bf16[1,64,3072]{2,1,0:T(8,128)(2,1)} %fusion.63) | copy-start | bytes 1179652
  284.0 54.8 %copy-start.1 = (bf16[1,448,3072]{2,1,0:T(8,128)(2,1)S(1)}, bf16[1,448,3072]{2,1,0:T(8,128)(2,1)}, u32[]{:S(2)}) copy-start(bf16[1,448,3072]{2,1,0:T(8,128)(2,1)} %all-gather.10.cloned.1.call-done) | copy-start | bytes 8257540
  351.0 4.7 copy-start.29
  351.0 4.7 copy-start.30
  354.7 2.9 copy-start.22
  354.7 2.9 copy-start.25
  355.6 2.0 copy-start.10
  355.6 2.0 copy-start.35
  377.6 4.3 copy-start.16
  381.0 0.8 copy-start.6
  381.1 1.6 copy-start.8
  384.5 139.8 %reduce-scatter.5.cloned.1.call-start = ((), (), s32[]{:S(2)}) async-start(), calls=%async_computation.8 | async-start | bytes 3932160 | tf_op jit(solution)/shard_map/reduce_scatter | solution.py:116
  399.1 10.1 %copy-start.13 = (bf16[3072,512,1]{1,0,2:T(8,128)(2,1)S(1)}, bf16[3072,512,1]{1,0,2:T(8,128)(2,1)}, u32[]{:S(2)}) copy-start(bf16[3072,512,1]{1,0,2:T(8,128)(2,1)} %reshape.259) | copy-start | bytes 9437188
  412.2 1.9 copy-start.7
  412.2 1.9 copy-start.9
  412.2 1.9 copy-start.17
  414.0 1.1 copy-start.12
  414.0 1.1 copy-start.21
  414.1 173.9 %reduce-scatter.7.cloned.1.call-start = ((), (), s32[]{:S(2)}) async-start(), calls=%async_computation.11 | async-start | bytes 17694720
  414.3 1.8 copy-start.15
  414.3 1.8 copy-start.31
  414.3 2.5 copy-start.40
  415.1 3.6 copy-start.19
  416.9 1.8 copy-start.2
  416.9 1.9 copy-start.33
  416.9 1.9 copy-start.34
  416.9 1.9 copy-start.38
  452.6 1.0 copy-start.5
  475.9 24.2 %copy-start.11 = (bf16[64,3,4,128]{0,3,2,1:T(8,128)(2,1)S(1)}, bf16[64,3,4,128]{0,3,2,1:T(8,128)(2,1)}, u32[]{:S(2)}) copy-start(bf16[64,3,4,128]{0,3,2,1:T(8,128)(2,1)} %pad_maximum_fusion.5) | copy-start | bytes 589828
  500.1 7.3 %copy-start.20 = (bf16[448,3,4,128]{0,3,2,1:T(8,128)(2,1)S(1)}, bf16[448,3,4,128]{0,3,2,1:T(8,128)(2,1)}, u32[]{:S(2)}) copy-start(bf16[448,3,4,128]{0,3,2,1:T(8,128)(2,1)} %copy-done.19) | copy-start | bytes 4128772
  500.1 7.4 %copy-start.39 = (f32[448]{0:T(512)S(1)}, f32[448]{0:T(512)}, u32[]{:S(2)}) copy-start(f32[448]{0:T(512)} %add_rsqrt_fusion.2) | copy-start | bytes 5380
  507.4 9.6 %copy-start.18 = (bf16[1,64,8,384]{3,1,2,0:T(8,128)(2,1)S(1)}, bf16[1,64,8,384]{3,1,2,0:T(8,128)(2,1)}, u32[]{:S(2)}) copy-start(bf16[1,64,8,384]{3,1,2,0:T(8,128)(2,1)} %copy.74) | copy-start | bytes 1179652
  522.4 3.2 copy-start.24
  522.4 3.9 copy-start.14
  522.4 3.9 copy-start.32
  593.4 3.6 copy-start.3
Sparse Core Ops, SparseCore 0:
  9.6 68.0 all-gather.9
  79.5 31.1 all-gather.13
  112.6 32.1 all-gather.15
  146.3 56.9 all-gather.17
  204.9 57.4 all-gather.7
  264.1 58.6 all-gather.11
  384.6 25.6 all-gather.19
  414.2 60.3 reduce-scatter.4
  478.1 109.8 reduce-scatter.6
where the time goes:
time: 612 us; the launch traced here: 606 us
  waiting for transfers between devices  264 us (43%)
  local copies, waits for them, and re-layouts  126 us (21%)
  matrix products  84.2 us (14%)
  blocking collectives  70.6 us (12%)
  other arithmetic  46.6 us (8%)
  between operations  14.7 us (2%)
    all_gather x1, waiting for transfers between devices, body(): lax.all_gather(text_qkv_weight, 'dp', axis=0, tiled=True)  54.1 us
    unnamed x93, local copies, waits for them, and re-layouts  51.8 us
    all_gather x1, waiting for transfers between devices, body(): lax.all_gather(image_slope, 'context', axis=1, tiled=True)  46.9 us
    unnamed x10, waiting for transfers between devices  43.6 us
    all_gather x1, waiting for transfers between devices, body(): lax.all_gather(image_qkv_weight, 'dp', axis=0, tiled=True)  38.9 us
    all_gather x1, waiting for transfers between devices, body(): lax.all_gather(text_out_weight, 'dp', axis=0, tiled=True)  29 us
    all_gather x1, waiting for transfers between devices, body(): lax.all_gather(image_out_weight, 'dp', axis=0, tiled=True)  26.6 us
    all_gather x1, waiting for transfers between devices, body(): lax.all_gather(image_tokens, 'context', axis=1, tiled=True)  24.9 us
  transfers between devices with their start and end apart: 9, of which 7 were waited for; matrix products, arithmetic and copies ran while one was open for 30% of the time, Pallas kernels for 0%

commit v1 on v0

--- a/solution.py
+++ b/solution.py
@@ -4,6 +4,19 @@
 from jax.sharding import PartitionSpec as P
 
 norm_eps = 1e-06
+
+
+def ring_gather(x, axis, dim):
+    devices, position, extent = (lax.axis_size(axis), lax.axis_index(axis), x.shape[dim])
+    ahead = [(i, (i + 1) % devices) for i in range(devices)]
+    out = jnp.zeros((*x.shape[:dim], devices * extent, *x.shape[dim + 1 :]), x.dtype)
+    held = x
+    for hop in range(devices):
+        source = (position - hop) % devices
+        out = lax.dynamic_update_slice_in_dim(out, held, source * extent, axis=dim)
+        if hop < devices - 1:
+            held = lax.ppermute(held, axis, ahead)
+    return out
 
 
 def layer_normal(values):
@@ -71,7 +84,7 @@
     )
     full_q_image, full_q_text, full_o_image, full_o_text = (
         lax.all_gather(image_qkv_weight, "dp", axis=0, tiled=True),
-        lax.all_gather(text_qkv_weight, "dp", axis=0, tiled=True),
+        ring_gather(text_qkv_weight, "dp", 0),
         lax.all_gather(image_out_weight, "dp", axis=0, tiled=True),
         lax.all_gather(text_out_weight, "dp", axis=0, tiled=True),
     )

time: 612 us -> 567 us (0.926)
  waiting for transfers between devices: 264 us -> 196 us
  local copies, waits for them, and re-layouts: 126 us -> 142 us
    ppermute x0 -> x7, waiting for transfers between devices: none -> 89.5 us  [ring_gather(): held = lax.ppermute(held, axis, ahead)]
    all_gather x1 -> x0, waiting for transfers between devices: 54.1 us -> none  [body(): lax.all_gather(text_qkv_weight, 'dp', axis=0, tiled=True)]
    all_gather x1, waiting for transfers between devices: 29 us -> 0.01 us  [body(): lax.all_gather(text_out_weight, 'dp', axis=0, tiled=True)]
    all_gather x1, waiting for transfers between devices: 26.6 us -> 0.01 us  [body(): lax.all_gather(image_out_weight, 'dp', axis=0, tiled=True)]
    all_gather x1, waiting for transfers between devices: 24.9 us -> 0.01 us  [body(): lax.all_gather(image_tokens, 'context', axis=1, tiled=True)]
    all_gather x1, waiting for transfers between devices: 38.9 us -> 23.2 us  [body(): lax.all_gather(image_qkv_weight, 'dp', axis=0, tiled=True)]
    dynamic_update_slice x0 -> x8, local copies, waits for them, and re-layouts: none -> 15.4 us  [ring_gather(): out = lax.dynamic_update_slice_in_dim(out, held, source * extent, axis=dim)]
    all_gather x1, waiting for transfers between devices: 46.9 us -> 40.3 us  [body(): lax.all_gather(image_slope, 'context', axis=1, tiled=True)]
  transfers between devices with their start and end apart: 9 -> 15, of which waited for: 7 -> 8; matrix products, arithmetic and copies ran while one was open for 30% -> 36% of each run, Pallas kernels for 0% -> 0%
where the time goes in v1:
time: 567 us; the launch traced here: 560 us
  waiting for transfers between devices  196 us (35%)
  local copies, waits for them, and re-layouts  142 us (25%)
  matrix products  84.7 us (15%)
  blocking collectives  72 us (13%)
  other arithmetic  48.1 us (8%)
  between operations  15 us (3%)
    ppermute x7, waiting for transfers between devices, ring_gather(): held = lax.ppermute(held, axis, ahead)  89.5 us
    unnamed x95, local copies, waits for them, and re-layouts  51.2 us
    unnamed x9, waiting for transfers between devices  43 us
    all_gather x1, waiting for transfers between devices, body(): lax.all_gather(image_slope, 'context', axis=1, tiled=True)  40.3 us
    all_gather x1, waiting for transfers between devices, body(): lax.all_gather(image_qkv_weight, 'dp', axis=0, tiled=True)  23.2 us
    dot_general x4, matrix products, contract_last(): lax.dot_general(left_side, right_side, (((1,), (1,)), ((), ())), preferre...  22.8 us
    all_gather x1, blocking collectives, body(): lax.all_gather(text_tokens, 'context', axis=1, tiled=True)  21 us
    psum x1, blocking collectives, body(): lax.psum(part_image.astype(jnp.bfloat16), 'context').astype(jnp.float32)  19.3 us
  transfers between devices with their start and end apart: 15, of which 8 were waited for; matrix products, arithmetic and copies ran while one was open for 36% of the time, Pallas kernels for 0%

profile of v1, /device:TPU:0, one launch (start us, length us, event | category | flops | bytes accessed | tf_op | source)
XLA Modules:
  0.0 559.7 jit_solution(870199572671521147)
XLA Ops:
  11.1 17.0 %collective-permute-done = bf16[384,3,4,128]{3,2,1,0:T(4,128)(2,1)S(1)} collective-permute-done((bf16[384,3,4,128]{3,2,1,0:T(4,128)(2,1)}, bf16[384,3,4,128]{3,2,1,0:T(4,128)(2,1)S(1)}, u32[]{:S(2)}, u32[]{:S(2)}) %collective-permute-start) | collective-permute-done | bytes 1179680 | tf_op jit(solution)/shard_map/ppermute | solution.py:18
  29.6 21.0 %all_gather.24 = bf16[1,64,3072]{2,1,0:T(8,128)(2,1)S(1)} all-gather(bf16[1,16,3072]{2,1,0:T(8,128)(2,1)} %param.11), channel_id=1, replica_groups=mesh['dp'=8,'context'=4] {'context'}, dimensions={1}, use_global_device_ids=true | all-gather | bytes 491520 | tf_op jit(solution)/shard_map/all_gather | solution.py:81
  50.8 4.1 broadcast_in_dim.18
  54.8 1.5 constant_dynamic-update-slice_fusion.7
  56.3 19.1 %all_gather.29 = bf16[1,64,3072]{2,1,0:T(8,128)(2,1)} all-gather(bf16[1,16,3072]{2,1,0:T(8,128)(2,1)S(1)} %copy-done.25), channel_id=1, replica_groups=mesh['dp'=8,'context'=4] {'context'}, dimensions={1}, use_global_device_ids=true | all-gather | bytes 491520 | tf_op jit(solution)/shard_map/all_gather | solution.py:83
  75.5 16.5 %collective-permute-done.2 = bf16[384,3,4,128]{3,2,1,0:T(4,128)(2,1)S(1)} collective-permute-done((bf16[384,3,4,128]{3,2,1,0:T(4,128)(2,1)S(1)}, bf16[384,3,4,128]{3,2,1,0:T(4,128)(2,1)S(1)}, u32[]{:S(2)}, u32[]{:S(2)}) %collective-permute-start.2) | collective-permute-done | bytes 1179680 | tf_op jit(solution)/shard_map/ppermute | solution.py:18
  93.2 23.0 %collective-permute-done.3 = bf16[384,3,4,128]{3,2,1,0:T(4,128)(2,1)S(1)} collective-permute-done((bf16[384,3,4,128]{3,2,1,0:T(4,128)(2,1)S(1)}, bf16[384,3,4,128]{3,2,1,0:T(4,128)(2,1)S(1)}, u32[]{:S(2)}, u32[]{:S(2)}) %collective-permute-start.3) | collective-permute-done | bytes 1179680 | tf_op jit(solution)/shard_map/ppermute | solution.py:18
  117.4 1.4 constant_dynamic-update-slice_fusion.6
  118.9 14.8 %collective-permute-done.4 = bf16[384,3,4,128]{3,2,1,0:T(4,128)(2,1)} collective-permute-done((bf16[384,3,4,128]{3,2,1,0:T(4,128)(2,1)S(1)}, bf16[384,3,4,128]{3,2,1,0:T(4,128)(2,1)}, u32[]{:S(2)}, u32[]{:S(2)}) %collective-permute-start.4) | collective-permute-done | bytes 1179680 | tf_op jit(solution)/shard_map/ppermute | solution.py:18
  136.5 2.4 convert_reduce_fusion.1
  140.6 18.4 %collective-permute-done.5 = bf16[384,3,4,128]{3,2,1,0:T(4,128)(2,1)} collective-permute-done((bf16[384,3,4,128]{3,2,1,0:T(4,128)(2,1)}, bf16[384,3,4,128]{3,2,1,0:T(4,128)(2,1)}, u32[]{:S(2)}, u32[]{:S(2)}) %collective-permute-start.5) | collective-permute-done | bytes 1179680 | tf_op jit(solution)/shard_map/ppermute | solution.py:18
  160.5 2.4 copy.102
  163.0 3.1 copy.89
  166.1 4.5 copy.103
  170.6 3.2 copy.88
  173.7 2.7 convolution_convert_fusion.8
  176.4 40.3 %all-gather.15.cloned.1.call-done = bf16[1,448,3072]{2,1,0:T(8,128)(2,1)} async-done(((bf16[1,112,3072]{2,1,0:T(8,128)(2,1)}), bf16[1,448,3072]{2,1,0:T(8,128)(2,1)}) %all-gather.15.cloned.1.call-update) | async-done | bytes 2752528 | tf_op jit(solution)/shard_map/all_gather | solution.py:82
  216.7 5.1 fusion.49
  221.8 2.7 constant_dynamic-update-slice_fusion.2
  224.5 2.9 constant_dynamic-update-slice_fusion.1
  227.4 2.7 constant_dynamic-update-slice_fusion
  230.1 16.0 %reshape.247 = bf16[3072,1536]{1,0:T(8,128)(2,1)} reshape(bf16[3072,3,4,128]{3,2,1,0:T(4,128)(2,1)} %constant_dynamic-update-slice_fusion) | data formatting | bytes 18874368 | tf_op jit(solution)/shard_map/reshape | solution.py:92
  246.1 6.6 %fusion.78 = f32[64,1536]{1,0:T(8,128)S(1)} fusion(bf16[3072,1536]{1,0:T(8,128)(2,1)} %reshape.247, bf16[1,64,3072]{2,1,0:T(8,128)(2,1)S(1)} %copy-done.3), kind=kOutput, calls=%fused_computation.104 | convolution fusion | flops 603979776 | bytes 10223616 | tf_op jit(solution)/shard_map/dot_general | solution.py:99
  252.7 23.2 %all-gather.9.cloned.1.call-done = bf16[3072,3,4,128]{3,2,1,0:T(4,128)(2,1)} async-done(((bf16[384,3,4,128]{3,2,1,0:T(4,128)(2,1)}), bf16[3072,3,4,128]{3,2,1,0:T(4,128)(2,1)}) %all-gather.9.cloned.1.call-update) | async-done | bytes 9437200 | tf_op jit(solution)/shard_map/all_gather | solution.py:86
  275.9 15.9 %reshape.248 = bf16[3072,1536]{1,0:T(8,128)(2,1)} reshape(bf16[3072,3,4,128]{3,2,1,0:T(4,128)(2,1)} %all-gather.9.cloned.1.call-done) | data formatting | bytes 18874368 | tf_op jit(solution)/shard_map/reshape | solution.py:91
  291.8 7.6 %fusion.21 = f32[448,1536]{1,0:T(8,128)S(1)} fusion(bf16[3072,1536]{1,0:T(8,128)(2,1)} %reshape.248, bf16[1,448,3072]{2,1,0:T(8,128)(2,1)S(1)} %copy-done.1, f32[3072]{0:T(1024)} %bitcast.215, f32[448]{0:T(512)} %add_rsqrt_fusion.2, f32[448]{0:T(512)S(1)} %broadcast_multiply_fusion.2, f32[3072]{0:T(1024)} %bitcast.213), kind=kOutput, calls=%fused_computation.37 | convolution fusion | flops 4236115968 | bytes 14970368 | tf_op jit(solution)/shard_map/dot_general | solution.py:100
  299.4 1.9 pad_maximum_fusion.1
  301.3 2.6 copy.94
  304.2 3.8 fusion.80
  309.5 1.9 copy-done.9
  311.4 1.8 fusion.53
  313.2 8.0 %fusion.46 = f32[512,4,128]{0,2,1:T(8,128)} fusion(f32[4,512,512]{1,2,0:T(8,128)} %fusion.80, f32[512,3,4,128]{0,3,2,1:T(8,128)S(1)} %bitcast.182, f32[512,4]{0,1:T(4,128)} %copy-done.31, f32[4,512,512]{1,2,0:T(8,128)} %copy-done.9, f32[4,512]{1,0:T(4,128)} %copy-done.36), kind=kOutput, calls=%fused_computation.58 | convolution fusion | flops 278399488 | bytes 18898944 | tf_op jit(solution)/shard_map/hij,ihe->jhe/dot_general | solution.py:163
  321.2 10.0 %multiply_reduce_fusion.2 = (f32[512,4]{0,1:T(4,128)}, f32[512,4]{0,1:T(4,128)}, f32[512,4,128]{0,2,1:T(8,128)}) fusion(f32[512,3,4,128]{0,3,2,1:T(8,128)S(1)} %bitcast.183, f32[512,4]{0,1:T(4,128)} %copy-done.31, f32[512,4,128]{0,2,1:T(8,128)} %fusion.46, f32[512,4]{0,1:T(4,128)} %copy-done.30, f32[4,512,512]{1,2,0:T(8,128)} %fusion.80, ...), kind=kOutput, calls=%fused_computation.74 | convolution fusion | flops 279968256 | bytes 22077440 | tf_op jit(solution)/shard_map/hij,jhe->ihe/dot_general | solution.py:162
  332.7 2.0 fusion.71
  336.3 1.8 copy.75
  338.2 5.7 %reshape.258 = bf16[3072,512,1]{1,0,2:T(8,128)(2,1)} reshape(bf16[3072,4,128]{2,1,0:T(4,128)(2,1)} %all-gather.11.cloned.1.call-done) | data formatting | bytes 6291456 | tf_op jit(solution)/shard_map/reshape | solution.py:94
  343.9 5.8 %reshape.259 = bf16[3072,512,1]{1,0,2:T(8,128)(2,1)} reshape(bf16[3072,4,128]{2,1,0:T(4,128)(2,1)} %all-gather.13.cloned.1.call-done) | data formatting | bytes 6291456 | tf_op jit(solution)/shard_map/reshape | solution.py:93
  349.6 3.0 fusion.52
  354.4 1.6 copy.63
  356.1 1.5 dot_general.70
  357.6 2.2 reshape.263
  359.7 3.0 convolution_convert_fusion.5
  362.8 3.0 convolution_convert_fusion.4
  365.8 1.8 pad_maximum_fusion.2
  370.9 1.8 convolution_convert_fusion.3
  372.8 5.7 %convolution_convert_fusion = bf16[3072,1536]{0,1:T(8,128)(2,1)S(1)} fusion(bf16[448,1536]{0,1:T(8,128)(2,1)S(1)} %bitcast.202, bf16[1,448,3072]{2,1,0:T(8,128)(2,1)S(1)} %copy-done.2, f32[3072]{0:T(1024)S(1)} %bitcast.216, f32[448]{0:T(512)S(1)} %copy-done.39, f32[3072]{0:T(1024)S(1)} %bitcast.214, f32[448]{0:T(512)S(1)} %broadcast_multiply_fusion.2), kind=kOutput, calls=%fused_computation.3 | convolution fusion | flops 4240834560 | bytes 13594112 | tf_op jit(solution)/shard_map/dot_general | solution.py:44
  378.6 7.7 %pad_maximum_fusion = bf16[3072,2560]{0,1:T(8,128)(2,1)} fusion(bf16[3072,512]{0,1:T(8,128)(2,1)S(1)} %convolution_convert_fusion.2, bf16[3072,512]{0,1:T(8,128)(2,1)S(1)} %convolution_convert_fusion.3, bf16[3072,1536]{0,1:T(8,128)(2,1)S(1)} %convolution_convert_fusion), kind=kLoop, calls=%fused_computation.2 | loop fusion | flops 47185920 | bytes 31457280 | tf_op jit(solution)/shard_map/concatenate | solution.py:198
  386.2 19.7 %copy.92 = bf16[3072,2560]{1,0:T(8,128)(2,1)} copy(bf16[3072,2560]{0,1:T(8,128)(2,1)} %pad_maximum_fusion) | data formatting | bytes 31457280
  406.9 2.9 copy.72
  410.4 18.9 %reduce.2 = bf16[3072,64]{1,0:T(8,128)(2,1)} reduce(bf16[3072,1,64]{2,1,0:T(2,128)(2,1)} %bitcast.193, bf16[]{:T(256)} %broadcast.217), dimensions={1}, to_apply=%bitcast.152.reduce_sub_computation | reduce | bytes 786434
  429.2 2.7 reshape.268
  432.0 12.6 %all_to_all.18 = bf16[8,2,12288]{2,1,0:T(2,128)(2,1)} all-to-all(bf16[8,2,12288]{2,1,0:T(2,128)(2,1)} %reshape.268), channel_id=1, replica_groups=mesh['dp'=8,'context'=4] {'dp'}, dimensions={0} | all-to-all | bytes 786432 | tf_op jit(solution)/shard_map/all_to_all | solution.py:202
  444.6 3.8 reshape.269
  448.3 2.8 copy.95
  451.1 2.4 copy.74
  453.6 7.3 %fusion.103 = (bf16[3072]{0:T(1024)(128)(2,1)S(1)}, bf16[3072]{0:T(1024)(128)(2,1)S(1)}) fusion(f32[64]{0:T(128)} %copy-done.38, f32[64]{0:T(128)} %copy-done.37, bf16[1,64,3072]{2,1,0:T(8,128)(2,1)S(1)} %all_gather.24, bf16[64,1536]{0,1:T(8,128)(2,1)S(1)} %bitcast.196, bf16[3072,1536]{1,0:T(8,128)(2,1)} %reshape.247), kind=kOutput, calls=%fused_computation.139 | convolution fusion | flops 605153280 | bytes 10039808 | tf_op jit(solution)/shard_map/dot_general | solution.py:50
  461.0 9.5 %fusion.102 = (bf16[3072]{0:T(1024)(128)(2,1)S(1)}, bf16[3072]{0:T(1024)(128)(2,1)S(1)}) fusion(f32[448]{0:T(512)S(1)} %copy-done.40, f32[448]{0:T(512)S(1)} %broadcast_multiply_fusion.2, bf16[1,448,3072]{2,1,0:T(8,128)(2,1)S(1)} %copy-done.2, bf16[448,1536]{0,1:T(8,128)(2,1)S(1)} %bitcast.203, bf16[3072,1536]{1,0:T(8,128)(2,1)} %reshape.248), kind=kOutput, calls=%fused_computation.138 | convolution fusion | flops 4236109824 | bytes 13581824 | tf_op jit(solution)/shard_map/dot_general | solution.py:50
  470.5 4.0 convolution_convert_fusion.1
  475.9 1.9 reshape.253
  481.1 19.3 %all-reduce = (bf16[1,3,3072]{2,0,1:T(2,128)(2,1)S(1)}, bf16[1,3,3072]{2,0,1:T(2,128)(2,1)S(1)}) all-reduce(bf16[1,3,3072]{2,0,1:T(2,128)(2,1)S(1)} %broadcast_in_dim.41, bf16[1,3,3072]{2,0,1:T(2,128)(2,1)S(1)} %broadcast_in_dim.43), channel_id=1, replica_groups=mesh['dp'=8,'context'=4] {'context'}, use_global_device_ids=true, to_apply=%region_16.17 | all-reduce | flops 18432 | bytes 73728 | tf_op jit(solution)/shard_map/psum | solution.py:191
  501.7 39.8 %reduce-scatter.7.cloned.1.call-done = bf16[384,2560]{1,0:T(8,128)(2,1)} async-done(((bf16[3072,2560]{1,0:T(8,128)(2,1)}), bf16[384,2560]{1,0:T(8,128)(2,1)}) %reduce-scatter.7.cloned.1.call-update) | async-done | bytes 1966096
  541.6 2.8 copy.93
  544.4 1.6 slice.114
  546.1 4.3 copy.76
  (161 shorter events, 33.9 us)
Async XLA Ops:
  7.2 129.4 %all-gather.7.cloned.1.call-start = ((), (), s32[]{:S(2)}) async-start(), calls=%async_computation.3 | async-start | bytes 3440640 | tf_op jit(solution)/shard_map/all_gather | solution.py:80
  7.9 152.6 %all-gather.13.cloned.1.call-start = ((), (), s32[]{:S(2)}) async-start(), calls=%async_computation.6 | async-start | bytes 3538944 | tf_op jit(solution)/shard_map/all_gather | solution.py:88
  8.6 157.4 %all-gather.11.cloned.1.call-start = ((), (), s32[]{:S(2)}) async-start(), calls=%async_computation.5 | async-start | bytes 3538944 | tf_op jit(solution)/shard_map/all_gather | solution.py:89
  9.4 207.3 %all-gather.15.cloned.1.call-start = ((), (), s32[]{:S(2)}) async-start(), calls=%async_computation.8 | async-start | bytes 3440640 | tf_op jit(solution)/shard_map/all_gather | solution.py:82
  10.0 265.9 %all-gather.9.cloned.1.call-start = ((), (), s32[]{:S(2)}) async-start(), calls=%async_computation.4 | async-start | bytes 10616832 | tf_op jit(solution)/shard_map/all_gather | solution.py:86
  10.5 460.0 %all-gather.17.cloned.1.call-start = ((), (), s32[]{:S(2)}) async-start(), calls=%async_computation.9 | async-start | bytes 1769472 | tf_op jit(solution)/shard_map/all_gather | solution.py:203
  10.6 17.5 %collective-permute-start = (bf16[384,3,4,128]{3,2,1,0:T(4,128)(2,1)}, bf16[384,3,4,128]{3,2,1,0:T(4,128)(2,1)S(1)}, u32[]{:S(2)}, u32[]{:S(2)}) collective-permute-start(bf16[384,3,4,128]{3,2,1,0:T(4,128)(2,1)} %param.15), channel_id=1, source_target_pairs={{0,4},{4,8},{8,12},{12,16},{16,20},{20,24},{24,28},{28,0},{1,5},{5... | collective-permute-start | bytes 3538952 | tf_op jit(solution)/shard_map/ppermute | solution.py:18
  28.1 47.3 %collective-permute-start.1 = (bf16[384,3,4,128]{3,2,1,0:T(4,128)(2,1)S(1)}, bf16[384,3,4,128]{3,2,1,0:T(4,128)(2,1)S(1)}, u32[]{:S(2)}, u32[]{:S(2)}) collective-permute-start(bf16[384,3,4,128]{3,2,1,0:T(4,128)(2,1)S(1)} %collective-permute-done), channel_id=1, source_target_pairs={{0,4},{4,8},{8,12},{12,16},{16,20},{20,24},{24,28},{28,0},{1,5},{5... | collective-permute-start | bytes 3538952 | tf_op jit(solution)/shard_map/ppermute | solution.py:18
  50.7 4.1 copy-start.20
  50.7 5.6 copy-start.25
  50.8 24.7 %copy-start.28 = (bf16[1,3,3072]{2,1,0:T(4,128)(2,1)S(1)}, bf16[1,3,3072]{2,1,0:T(4,128)(2,1)}, u32[]{:S(2)}) copy-start(bf16[1,3,3072]{2,1,0:T(4,128)(2,1)} %param.13) | copy-start | bytes 55300
  50.8 41.2 %copy-start.29 = (bf16[1,3,3072]{2,1,0:T(4,128)(2,1)S(1)}, bf16[1,3,3072]{2,1,0:T(4,128)(2,1)}, u32[]{:S(2)}) copy-start(bf16[1,3,3072]{2,1,0:T(4,128)(2,1)} %param.12) | copy-start | bytes 55300
  75.4 61.1 %copy-start.37 = (f32[64]{0:T(128)}, f32[64]{0:T(128)S(1)}, u32[]{:S(2)}) copy-start(f32[64]{0:T(128)S(1)} %broadcast_multiply_fusion.3) | copy-start | bytes 772
  75.4 16.6 %collective-permute-start.2 = (bf16[384,3,4,128]{3,2,1,0:T(4,128)(2,1)S(1)}, bf16[384,3,4,128]{3,2,1,0:T(4,128)(2,1)S(1)}, u32[]{:S(2)}, u32[]{:S(2)}) collective-permute-start(bf16[384,3,4,128]{3,2,1,0:T(4,128)(2,1)S(1)} %collective-permute-done.1), channel_id=1, source_target_pairs={{0,4},{4,8},{8,12},{12,16},{16,20},{20,24},{24,28},{28,0},{1,5},{5... | collective-permute-start | bytes 3538952 | tf_op jit(solution)/shard_map/ppermute | solution.py:18
  92.0 24.2 %collective-permute-start.3 = (bf16[384,3,4,128]{3,2,1,0:T(4,128)(2,1)S(1)}, bf16[384,3,4,128]{3,2,1,0:T(4,128)(2,1)S(1)}, u32[]{:S(2)}, u32[]{:S(2)}) collective-permute-start(bf16[384,3,4,128]{3,2,1,0:T(4,128)(2,1)S(1)} %collective-permute-done.2), channel_id=1, source_target_pairs={{0,4},{4,8},{8,12},{12,16},{16,20},{20,24},{24,28},{28,0},{1,5},{5... | collective-permute-start | bytes 3538952 | tf_op jit(solution)/shard_map/ppermute | solution.py:18
  116.2 18.9 %copy-start.21 = (bf16[384,3,4,128]{3,2,1,0:T(4,128)(2,1)}, bf16[384,3,4,128]{3,2,1,0:T(4,128)(2,1)S(1)}, u32[]{:S(2)}) copy-start(bf16[384,3,4,128]{3,2,1,0:T(4,128)(2,1)S(1)} %collective-permute-done.3) | copy-start | bytes 3538948
  116.2 17.5 %collective-permute-start.4 = (bf16[384,3,4,128]{3,2,1,0:T(4,128)(2,1)S(1)}, bf16[384,3,4,128]{3,2,1,0:T(4,128)(2,1)}, u32[]{:S(2)}, u32[]{:S(2)}) collective-permute-start(bf16[384,3,4,128]{3,2,1,0:T(4,128)(2,1)S(1)} %collective-permute-done.3), channel_id=1, source_target_pairs={{0,4},{4,8},{8,12},{12,16},{16,20},{20,24},{24,28},{28,0},{1,5},{5... | collective-permute-start | bytes 3538952 | tf_op jit(solution)/shard_map/ppermute | solution.py:18
  116.5 22.4 %copy-start.38 = (f32[64]{0:T(128)}, f32[64]{0:T(128)S(1)}, u32[]{:S(2)}) copy-start(f32[64]{0:T(128)S(1)} %add_rsqrt_fusion.3) | copy-start | bytes 772
  133.7 25.3 %collective-permute-start.5 = (bf16[384,3,4,128]{3,2,1,0:T(4,128)(2,1)}, bf16[384,3,4,128]{3,2,1,0:T(4,128)(2,1)}, u32[]{:S(2)}, u32[]{:S(2)}) collective-permute-start(bf16[384,3,4,128]{3,2,1,0:T(4,128)(2,1)} %collective-permute-done.4), channel_id=1, source_target_pairs={{0,4},{4,8},{8,12},{12,16},{16,20},{20,24},{24,28},{28,0},{1,5},{5... | collective-permute-start | bytes 3538952 | tf_op jit(solution)/shard_map/ppermute | solution.py:18
  136.5 2.6 copy-start
  136.5 22.6 %copy-start.22 = (bf16[384,3,4,128]{3,2,1,0:T(4,128)(2,1)S(1)}, bf16[384,3,4,128]{3,2,1,0:T(4,128)(2,1)}, u32[]{:S(2)}) copy-start(bf16[384,3,4,128]{3,2,1,0:T(4,128)(2,1)} %copy-done.21) | copy-start | bytes 3538948
  158.9 68.5 %collective-permute-start.6 = (bf16[384,3,4,128]{3,2,1,0:T(4,128)(2,1)}, bf16[384,3,4,128]{3,2,1,0:T(4,128)(2,1)}, u32[]{:S(2)}, u32[]{:S(2)}) collective-permute-start(bf16[384,3,4,128]{3,2,1,0:T(4,128)(2,1)} %collective-permute-done.5), channel_id=1, source_target_pairs={{0,4},{4,8},{8,12},{12,16},{16,20},{20,24},{24,28},{28,0},{1,5},{5... | collective-permute-start | bytes 3538952 | tf_op jit(solution)/shard_map/ppermute | solution.py:18
  230.1 16.0 %copy-start.3 = (bf16[1,64,3072]{2,1,0:T(8,128)(2,1)S(1)}, bf16[1,64,3072]{2,1,0:T(8,128)(2,1)}, u32[]{:S(2)}) copy-start(bf16[1,64,3072]{2,1,0:T(8,128)(2,1)} %fusion.63) | copy-start | bytes 1179652
  252.7 39.1 %copy-start.1 = (bf16[1,448,3072]{2,1,0:T(8,128)(2,1)S(1)}, bf16[1,448,3072]{2,1,0:T(8,128)(2,1)}, u32[]{:S(2)}) copy-start(bf16[1,448,3072]{2,1,0:T(8,128)(2,1)} %all-gather.7.cloned.1.call-done) | copy-start | bytes 8257540
  307.9 3.5 copy-start.24
  307.9 3.5 copy-start.27
  308.0 0.6 copy-start.30
  308.0 1.5 copy-start.31
  309.4 1.9 copy-start.9
  309.5 2.0 copy-start.36
  331.2 4.3 copy-start.15
  334.7 0.8 copy-start.5
  334.7 1.6 copy-start.7
  338.1 139.7 %reduce-scatter.5.cloned.1.call-start = ((), (), s32[]{:S(2)}) async-start(), calls=%async_computation.7 | async-start | bytes 3932160 | tf_op jit(solution)/shard_map/reduce_scatter | solution.py:129
  352.7 10.1 %copy-start.12 = (bf16[3072,512,1]{1,0,2:T(8,128)(2,1)S(1)}, bf16[3072,512,1]{1,0,2:T(8,128)(2,1)}, u32[]{:S(2)}) copy-start(bf16[3072,512,1]{1,0,2:T(8,128)(2,1)} %reshape.259) | copy-start | bytes 9437188
  365.7 2.4 copy-start.6
  365.8 2.4 copy-start.8
  365.8 2.4 copy-start.16
  367.6 1.5 copy-start.11
  367.6 1.5 copy-start.23
  367.7 173.9 %reduce-scatter.7.cloned.1.call-start = ((), (), s32[]{:S(2)}) async-start(), calls=%async_computation.10 | async-start | bytes 17694720
  368.4 1.8 copy-start.14
  368.4 1.8 copy-start.32
  368.4 2.5 copy-start.41
  369.1 3.6 copy-start.18
  370.9 1.8 copy-start.2
  370.9 1.9 copy-start.34
  370.9 1.9 copy-start.35
  370.9 1.9 copy-start.39
  405.9 1.0 copy-start.4
  429.2 24.4 %copy-start.10 = (bf16[64,3,4,128]{0,3,2,1:T(8,128)(2,1)S(1)}, bf16[64,3,4,128]{0,3,2,1:T(8,128)(2,1)}, u32[]{:S(2)}) copy-start(bf16[64,3,4,128]{0,3,2,1:T(8,128)(2,1)} %pad_maximum_fusion.5) | copy-start | bytes 589828
  453.6 7.4 %copy-start.19 = (bf16[448,3,4,128]{0,3,2,1:T(8,128)(2,1)S(1)}, bf16[448,3,4,128]{0,3,2,1:T(8,128)(2,1)}, u32[]{:S(2)}) copy-start(bf16[448,3,4,128]{0,3,2,1:T(8,128)(2,1)} %copy-done.18) | copy-start | bytes 4128772
  453.6 7.4 %copy-start.40 = (f32[448]{0:T(512)S(1)}, f32[448]{0:T(512)}, u32[]{:S(2)}) copy-start(f32[448]{0:T(512)} %add_rsqrt_fusion.2) | copy-start | bytes 5380
  461.0 9.5 %copy-start.17 = (bf16[1,64,8,384]{3,1,2,0:T(8,128)(2,1)S(1)}, bf16[1,64,8,384]{3,1,2,0:T(8,128)(2,1)}, u32[]{:S(2)}) copy-start(bf16[1,64,8,384]{3,1,2,0:T(8,128)(2,1)} %copy.74) | copy-start | bytes 1179652
  475.9 3.2 copy-start.26
  475.9 4.0 copy-start.13
  475.9 4.0 copy-start.33
Sparse Core Ops, SparseCore 0:
  9.5 72.0 all-gather.6
  83.5 36.6 all-gather.12
  122.1 37.1 all-gather.10
  160.7 56.0 all-gather.14
  218.4 57.4 all-gather.8
  338.2 25.6 all-gather.16
  367.8 60.3 reduce-scatter.4
  431.7 109.8 reduce-scatter.6
